TPU v7x, 256 devices: a whole 4x4x8 slice. The times are simulated.
256 devices in a mesh: tm: 8 (over z), lat: 4 (over x), lon: 8 (over y, core).
Axes of the slice: x: 4, y: 4, z: 8, core: 2. Of those that a mesh axis runs over, the one named last changes fastest.
Arguments:
- slab: bfloat16 [512, 262144], P('tm', ('lat', 'lon')), may hold values from -6 to 6
- start: bfloat16 [512, 64], P('tm'), may hold values from -6 to 6
- sections: float32 [3, 2], replicated, may hold values from 0.2 to 1.5708, as said below
Outputs:
- basis: float32 [2048, 64, 128], P(('lat', 'lon', 'tm'))
- pcs: float32 [512, 64], P('tm')
Inputs may be any that keep to these rules, and one draw needn't show every extreme that they name: `sections`: in each column, one section has radius 0.78 to 0.86 and angle 2 pi / 8 to 2 pi / 4, the other radius 0.9955 to 0.9985 and angle 2 pi / 24 to 2 pi / 12; which column is which varies; amplitudes 0.2 to 1.0.
All inputs are finite; a program needn't handle non-finite values.
Results may differ from a plain program's by a relative error of at most 0.0039.
Values may be sent and summed in bfloat16 or wider, within the bound.
A program may use at most 64 MiB of HBM per device.

v0:
```python
import math

import jax
import jax.numpy as jnp
from jax import lax
from jax.sharding import PartitionSpec as P

LANES = 128


TOP_PRECISION = lax.Precision.HIGHEST


def prefix(value, axis, join, neutral):
    count, mine = (lax.axis_size(axis), lax.axis_index(axis))
    pieces = jax.tree.map(lambda part: lax.all_gather(part, axis), value)
    running = jax.tree.map(
        lambda part, zero: jnp.full_like(part, 0) + jnp.asarray(zero, part.dtype), value, neutral
    )

    def step(position, running):
        longer = join(running, jax.tree.map(lambda part: part[position], pieces))
        return jax.tree.map(lambda new, old: jnp.where(position < mine, new, old), longer, running)

    return lax.fori_loop(0, count - 1, step, running)


def impulse(radius, angle, steps):
    counted = jnp.maximum(steps, 0).astype(jnp.float32)
    values = jnp.exp(counted * jnp.log(radius)) * jnp.sin((counted + 1.0) * angle) / jnp.sin(angle)
    return jnp.where(steps >= 0, values, 0.0)


def section_columns(radius, angle, feed_two, drive_gain, times):
    return [
        -drive_gain * impulse(radius, angle, times - 1),
        -drive_gain * impulse(radius, angle, times),
        impulse(radius, angle, times + 1),
        feed_two * impulse(radius, angle, times),
    ]


def block_maps(sections, hour_count):
    radius = sections[0]
    angles = sections[1]
    amplitude = sections[2]
    feed_two = -radius * radius
    drive_gain = amplitude * jnp.sqrt(1.0 - radius * radius)
    hours = jnp.arange(hour_count, dtype=jnp.int32)
    lag = hours[:, None] - hours[None, :]
    drive_rows = jnp.zeros((hour_count, hour_count), jnp.float32)
    input_rows = [
        (hours == hour_count - 1).astype(jnp.float32),
        (hours == hour_count - 2).astype(jnp.float32),
    ]
    state_parts = []
    end_rows = [jnp.zeros((6,), jnp.float32), jnp.zeros((6,), jnp.float32)]
    for section in range(2):
        rad = radius[section]
        ang = angles[section]
        drive_rows = drive_rows + drive_gain[section] * (
            impulse(rad, ang, lag) - impulse(rad, ang, lag - 2)
        )
        for back in range(2):
            ahead = hour_count - 1 - back - hours
            input_rows.append(
                drive_gain[section] * (impulse(rad, ang, ahead) - impulse(rad, ang, ahead - 2))
            )
        state_parts.append(section_columns(rad, ang, feed_two[section], drive_gain[section], hours))
        for back in range(2):
            moment = jnp.array(hour_count - 1 - back, jnp.int32)
            pieces = section_columns(rad, ang, feed_two[section], drive_gain[section], moment)
            zeros_pair = [jnp.zeros((), jnp.float32), jnp.zeros((), jnp.float32)]
            own = pieces[2:] + zeros_pair if section == 0 else zeros_pair + pieces[2:]
            end_rows.append(jnp.stack(pieces[:2] + own))
    first, second = state_parts
    state_rows = jnp.stack(
        [first[0] + second[0], first[1] + second[1], first[2], first[3], second[2], second[3]],
        axis=1,
    )
    end_inputs = jnp.stack(input_rows)
    end_state = jnp.stack(end_rows)
    return (drive_rows, end_inputs, state_rows, end_state)


def combine(earlier, subsequent):
    concatenated_rows = jnp.dot(subsequent[0], earlier[0], precision=TOP_PRECISION)
    vector = jnp.dot(subsequent[0], earlier[1], precision=TOP_PRECISION) + subsequent[1]
    return (concatenated_rows, vector)


def make_orthonormal(spatial_patterns):
    local_gram_block = jnp.einsum(
        "zrs,zts->rt", spatial_patterns, spatial_patterns, precision=TOP_PRECISION
    )
    gram_matrix = lax.psum(local_gram_block, ("tm", "lat", "lon"))
    lower_factor = jnp.linalg.cholesky(gram_matrix)
    width = gram_matrix.shape[0]
    inverse_factor = jax.scipy.linalg.solve_triangular(
        lower_factor, jnp.eye(width, dtype=jnp.float32), lower=True
    )
    return jnp.einsum("de,wes->wds", inverse_factor, spatial_patterns, precision=TOP_PRECISION)


def local(slab, start, sections):
    hour_count, cell_count = slab.shape
    width = start.shape[1]
    drive_rows, end_inputs, state_rows, end_state = block_maps(sections, hour_count)
    values = slab.astype(jnp.float32)
    local_part = jnp.dot(drive_rows, values, precision=TOP_PRECISION)
    leaving = jnp.dot(end_inputs, values, precision=TOP_PRECISION)
    identity_pair = (jnp.eye(6, dtype=jnp.float32), jnp.zeros_like(leaving))
    entering = prefix((end_state, leaving), "tm", combine, identity_pair)[1]
    filtered = (local_part + jnp.dot(state_rows, entering, precision=TOP_PRECISION)).astype(
        jnp.bfloat16
    )
    grouped = filtered.reshape(hour_count, cell_count // LANES, LANES)
    cells_all = cell_count * lax.axis_size("lat") * lax.axis_size("lon")
    hours_all = hour_count * lax.axis_size("tm")
    block_of_rows = grouped
    spatial_patterns = lax.psum_scatter(
        jnp.einsum("tk,tgc->gkc", start, block_of_rows, preferred_element_type=jnp.float32),
        "tm",
        scatter_dimension=0,
        tiled=True,
    )
    ortho = make_orthonormal(spatial_patterns)
    block_of_rows = grouped.astype(jnp.float32)
    partial_sums = jnp.zeros((hour_count, width), jnp.float32) + jnp.einsum(
        "tgc,gkc->tk",
        block_of_rows,
        lax.all_gather(ortho.astype(jnp.bfloat16), "tm", axis=0, tiled=True).astype(jnp.float32),
        precision=TOP_PRECISION,
    )
    projections = lax.psum(partial_sums, ("lat", "lon"))
    basis = ortho * math.sqrt(cells_all)
    pcs = projections * math.sqrt(hours_all / cells_all)
    return (basis, pcs)


def solution(mesh):
    return jax.shard_map(
        local,
        mesh=mesh,
        in_specs=(P("tm", ("lat", "lon")), P("tm", None), P()),
        out_specs=(P(("lat", "lon", "tm"), None, None), P("tm", None)),
        check_vma=False,
    )
```

profile of v0, /device:TPU:1, one launch (start us, length us, event | category | flops | bytes accessed | tf_op | source)
XLA Modules:
  0.0 375.0 jit_solution(5782166197295645485)
XLA Ops:
  7.2 1.0 slice_reduce_fusion
  8.2 1.5 fusion.87
  9.7 0.7 fusion.89
  13.1 1.4 fusion.80
  14.5 1.4 fusion.79
  15.9 1.2 convolution_bitcast_fusion
  20.7 0.7 fusion.88
  28.4 1.3 compare_select_fusion.9
  29.7 1.9 multiply_add_fusion.1
  31.7 1.3 compare_select_fusion.8
  33.0 25.0 %all-gather.2 = f32[8,6,6]{2,1,0:T(8,128)S(1)} all-gather(f32[1,6,6]{2,1,0:T(8,128)S(1)} %bitcast.79), channel_id=2, replica_groups=mesh['tm'=8,'lat'=4,'lon'=8] {'tm'}, dimensions={0}, use_global_device_ids=true | all-gather | bytes 1296 | tf_op jit(solution)/shard_map/all_gather | solution.py:16
  58.3 9.5 %while.14 = (s32[]{:T(128)}, f32[6,8192]{1,0:T(8,128)S(1)}, s32[]{:T(128)}, f32[8,6,6]{2,1,0:T(8,128)S(1)}, f32[8,6,8192]{2,1,0:T(8,128)}, /*index=5*/s32[]{:T(128)}, s32[]{:T(128)}) while((s32[]{:T(128)}, f32[6,8192]{1,0:T(8,128)S(1)}, s32[]{:T(128)}, f32[8,6,6]{2,1,0:T(8,128)S(1)}, f32[8,6,8192]{2,1,0:T(8,128)}, ...), condition=%wide.region_1.2_spmd.clone, body=%wide.region_0.1_spmd.clone.sunk | while | flops 3735556 | bytes 1317479 | solution.py:25
  58.3 1.3 fusion.106
  59.7 1.3 fusion.106
  61.1 1.3 fusion.106
  62.4 1.3 fusion.106
  63.8 1.3 fusion.106
  65.1 1.3 fusion.106
  66.5 1.3 fusion.106
  67.8 1.8 fusion.90
  69.7 4.2 %fusion.9 = bf16[8,64,8,128]{3,2,1,0:T(8,128)(2,1)S(1)} fusion(f32[64,8192]{1,0:T(8,128)S(1)} %fusion.90, bf16[64,8192]{1,0:T(8,128)(2,1)S(1)} %copy-done, f32[]{:T(128)S(6)} %sin.238, f32[]{:T(128)} %bitcast.5, f32[]{:T(128)} %bitcast.4, f32[]{:T(128)} %bitcast.3, f32[]{:T(128)S(6)} %sin.235, f32[]{:T(128)} %bitcast.2, f32[]{:T(128)} %bitcast.1, f32[]{:T(128)} %bitcast), kind=kOutput, calls=%fused_computation.13 | convolution fusion | flops 403845120 | bytes 4194336 | tf_op jit(solution)/shard_map/dot_general | solution.py:110
  73.9 1.8 convolution_bitcast_fusion.1
  75.8 41.6 %reduce-scatter.2.cloned.1.call-done = f32[8,64,128]{2,1,0:T(8,128)} async-done(((f32[64,64,128]{2,1,0:T(8,128)}), f32[8,64,128]{2,1,0:T(8,128)}) %reduce-scatter.2.cloned.1.call-update) | async-done | bytes 262160 | tf_op jit(solution)/shard_map/reduce_scatter | solution.py:121
  117.5 1.4 convolution_bitcast_fusion.4
  118.9 79.3 %psum.14 = f32[64,64]{0,1:T(8,128)S(1)} all-reduce(f32[64,64]{0,1:T(8,128)S(1)} %convolution_bitcast_fusion.4), channel_id=1, replica_groups=mesh['tm'=8,'lat'=4,'lon'=8] {'tm','lat','lon'}, use_global_device_ids=true, to_apply=%region_3.4 | all-reduce | flops 4096 | bytes 32768 | tf_op jit(solution)/shard_map/psum | solution.py:96
  198.2 5.8 %cholesky.16 = f32[64,64]{1,0:T(8,128)S(1)} custom-call(f32[64,64]{1,0:T(8,128)S(1)} %fusion.16), custom_call_target="Cholesky" | custom-call | tf_op jit(solution)/shard_map/jit(cholesky)/cholesky | solution.py:97
  204.8 0.7 fusion.14
  205.4 4.9 %custom-call.7 = f32[1,64,64]{1,2,0:T(8,128)S(1)} custom-call(f32[1,64,64]{2,1,0:T(8,128)S(1)} %fusion.14), custom_call_target="InvertDiagBlocksLowerTriangular" | custom-call | tf_op jit(solution)/shard_map/jit(_solve_triangular)/triangular_solve | solution.py:99
  210.6 2.1 convert_bitcast_fusion
  212.7 29.7 %all-gather.7.cloned.1.call-done = bf16[64,64,128]{2,1,0:T(8,128)(2,1)} async-done(((bf16[8,64,128]{2,1,0:T(8,128)(2,1)}), bf16[64,64,128]{2,1,0:T(8,128)(2,1)}) %all-gather.7.cloned.1.call-update) | async-done | bytes 1048592 | tf_op jit(solution)/shard_map/all_gather | solution.py:132
  242.4 1.6 convolution_bitcast_fusion.2
  244.1 123.8 %psum.15 = f32[64,64]{1,0:T(8,128)S(1)} all-reduce(f32[64,64]{1,0:T(8,128)S(1)} %convolution_bitcast_fusion.2), channel_id=1, replica_groups=mesh['tm'=8,'lat'=4,'lon'=8] {'lat','lon'}, use_global_device_ids=true, to_apply=%region_6.7 | all-reduce | flops 4096 | bytes 32768 | tf_op jit(solution)/shard_map/psum | solution.py:135
  (36 shorter events, 2.6 us)
Async XLA Ops:
  7.2 8.8 %copy-start = (bf16[64,8192]{1,0:T(8,128)(2,1)S(1)}, bf16[64,8192]{1,0:T(8,128)(2,1)}, u32[]{:S(2)}) copy-start(bf16[64,8192]{1,0:T(8,128)(2,1)} %param.5) | copy-start | bytes 3145732
  7.2 51.1 %all-gather.9.cloned.1.call-start = ((), (), s32[]{:S(2)}) async-start(), calls=%async_computation.3 | async-start | bytes 2359296 | tf_op jit(solution)/shard_map/all_gather | solution.py:16
  17.2 100.3 %reduce-scatter.2.cloned.1.call-start = ((), (), s32[]{:S(2)}) async-start(), calls=%async_computation.1 | async-start | bytes 2359296 | tf_op jit(solution)/shard_map/reduce_scatter | solution.py:121
  69.7 4.2 %copy-start.1 = (bf16[64,64]{1,0:T(8,128)(2,1)S(1)}, bf16[64,64]{1,0:T(8,128)(2,1)}, u32[]{:S(2)}) copy-start(bf16[64,64]{1,0:T(8,128)(2,1)} %param.6) | copy-start | bytes 24580
  75.8 166.7 %all-gather.7.cloned.1.call-start = ((), (), s32[]{:S(2)}) async-start(), calls=%async_computation.2 | async-start | bytes 1179648 | tf_op jit(solution)/shard_map/all_gather | solution.py:132
Sparse Core Ops, SparseCore 0:
  17.3 40.9 all-gather.8
  75.9 41.5 reduce-scatter.1
  212.8 29.5 all-gather.6
where the time goes:
time: 379 us; the launch traced here: 375 us
  blocking collectives  228 us (60%)
  waiting for transfers between devices  71.7 us (19%)
  between operations  26.8 us (7%)
  matrix products  23.6 us (6%)
  other arithmetic  20 us (5%)
  local copies, waits for them, and re-layouts  4.4 us (1%)
    psum x1, blocking collectives, local(): projections = lax.psum(partial_sums, ('lat', 'lon'))  124 us
    psum x1, blocking collectives, make_orthonormal(): gram_matrix = lax.psum(local_gram_block, ('tm', 'lat', 'lon'))  79.3 us
    reduce_scatter x1, waiting for transfers between devices, local(): lax.psum_scatter(jnp.einsum('tk,tgc->gkc', start, block_of_rows, preferre...  41.6 us
    all_gather x1, waiting for transfers between devices, local(): lax.all_gather(ortho.astype(jnp.bfloat16), 'tm', axis=0, tiled=True)  29.7 us
    all_gather x1, blocking collectives, prefix(): pieces = jax.tree.map(lambda part: lax.all_gather(part, axis), value)  25 us
    dot_general x7, matrix products, combine(): jnp.dot(subsequent[0], earlier[1], precision=TOP_PRECISION) + subsequent[1]  9.15 us
  transfers between devices with their start and end apart: 3, of which 3 were waited for; matrix products, arithmetic and copies ran while one was open for 1% of the time, Pallas kernels for 0%

commit v1 on v0

v1 whole, which is shorter than its diff:
```python
import functools
import math

import jax
import jax.numpy as jnp
from jax import lax
from jax.experimental import pallas as pl
from jax.experimental.pallas import tpu as pltpu
from jax.sharding import PartitionSpec as P

LANES = 128
BLOCK = 128
CHUNKS = 4
MESH = pl.DeviceIdType.MESH
FULL = lax.Precision.HIGHEST


def lane_rows(shape, axis):
    return lax.broadcasted_iota(jnp.int32, shape, axis)


def toeplitz_blocks(sections_ref, count):
    shape = (BLOCK, BLOCK)
    offset = lane_rows(shape, 0) - lane_rows(shape, 1)
    moment = offset.astype(jnp.float32)
    totals = [jnp.zeros(shape, jnp.float32) for _ in range(count)]
    at_zero = jnp.zeros((8, LANES), jnp.float32)
    for section in range(2):
        radius = jnp.full((8, LANES), sections_ref[0, section], jnp.float32)
        angle = jnp.full((8, LANES), sections_ref[1, section], jnp.float32)
        amplitude = jnp.full((8, LANES), sections_ref[2, section], jnp.float32)
        drive = amplitude * jnp.sqrt(1.0 - radius * radius)
        at_zero = at_zero + drive
        back = 1.0 / (radius * radius)
        sine, cosine = jnp.sin(angle), jnp.cos(angle)
        sine_part = drive * (1.0 - back) * cosine / sine
        cosine_part = drive * (1.0 + back)
        log_radius = jnp.log(radius)
        size = jnp.exp(moment * log_radius[:1])
        turn = moment * angle[:1]
        sine_of, cosine_of = size * jnp.sin(turn), size * jnp.cos(turn)
        for block in range(count):
            far = float(block * BLOCK)
            gain = jnp.exp(far * log_radius)
            far_sine, far_cosine = jnp.sin(far * angle), jnp.cos(far * angle)
            on_sine = gain * (sine_part * far_cosine - cosine_part * far_sine)
            on_cosine = gain * (sine_part * far_sine + cosine_part * far_cosine)
            totals[block] = totals[block] + on_sine[:1] * sine_of + on_cosine[:1] * cosine_of
    first = jnp.where(offset > 0, totals[0], jnp.where(offset == 0, at_zero[:1], 0.0))
    return [first] + totals[1:]


def factor_inverse(gram):
    width = gram.shape[0]
    count = width // 8
    rows = [gram[8 * m : 8 * m + 8] for m in range(count)]
    sub = lane_rows((8, LANES), 0)

    def spread(value, row):
        return jnp.broadcast_to(value[row : row + 1], (8, LANES))

    def step(position, rows):
        rows = list(rows)
        live = [(m < count - position).astype(jnp.float32) for m in range(count)]
        columns = [
            [jnp.broadcast_to(rows[m][:, j : j + 1], (8, LANES)) for m in range(count)] for j in range(8)
        ]
        head = rows[0]
        scale = jnp.ones((8, LANES), jnp.float32)
        scaled_rows = []
        for j in range(8):
            pivot = spread(columns[j][0], j)
            inverse_pivot = 1.0 / pivot
            scale = jnp.where(sub == j, lax.rsqrt(pivot), scale)
            columns[j][0] = jnp.where(sub > j, columns[j][0], 0.0)
            for k in range(j + 1, 8):
                weight = spread(columns[k][0], j) * inverse_pivot
                columns[k] = [ck - cj * weight for ck, cj in zip(columns[k], columns[j])]
            scaled = spread(head, j) * inverse_pivot
            scaled_rows.append(scaled)
            head = head - columns[j][0] * scaled
        out = []
        for m in range(1, count):
            taken = columns[0][m] * scaled_rows[0]
            for j in range(1, 8):
                taken = taken + columns[j][m] * scaled_rows[j]
            out.append(rows[m] - live[m] * taken)
        out.append(head * scale)
        return tuple(pltpu.roll(value, 2 * width - 8, 1) for value in out)

    rows = lax.fori_loop(0, count, step, tuple(rows))
    return jnp.concatenate(rows, axis=0)


def kernel(
    sizes,
    slab_ref, start_ref, sections_ref,
    basis_ref, pcs_ref,
    cells_ref, starts_ref, high_ref, low_ref, patterns_ref,
    gram_ref, gram_tm_ref, gram_xy_ref, gram_all_ref,
    shares_ref, shares_tm_ref, shares_xy_ref,
    local_sem, cells_send, cells_recv, starts_send, starts_recv,
    gram_send, gram_recv, shares_send, shares_recv,
    far_gram_send, far_gram_recv, far_shares_send, far_shares_recv,
    all_send, all_recv,
):
    tm_count, lat_count, lon_count, hour_count, width, own_cells = sizes
    hours_all = tm_count * hour_count
    chunk = own_cells // CHUNKS
    plane = lat_count * lon_count
    cells_all = own_cells * tm_count * plane
    tm, lat, lon = lax.axis_index("tm"), lax.axis_index("lat"), lax.axis_index("lon")
    here = lat * lon_count + lon
    order = sorted(range(1, tm_count), key=lambda d: -min(d, tm_count - d))

    barrier = pltpu.get_barrier_semaphore()

    def tm_peer(distance):
        return lax.rem(tm + distance, tm_count)

    def plane_peer(offset):
        other = lax.rem(lat + offset // lon_count, lat_count), lax.rem(lon + lax.rem(offset, lon_count), lon_count)
        return {"lat": other[0], "lon": other[1]}, other[0] * lon_count + other[1]

    for distance in order:
        pl.semaphore_signal(barrier, inc=1, device_id={"tm": tm_peer(distance)}, device_id_type=MESH)

    def greet(offset, carry):
        pl.semaphore_signal(barrier, inc=1, device_id=plane_peer(offset)[0], device_id_type=MESH)
        return carry

    lax.fori_loop(1, plane, greet, 0)

    def hours_of(index):
        return pl.ds(pl.multiple_of(index * hour_count, hour_count), hour_count)

    def cells_of(index, part):
        return pl.ds(pl.multiple_of(index * own_cells + part * chunk, chunk), chunk)

    own = [
        pltpu.make_async_copy(slab_ref.at[:, cells_of(tm, part)], cells_ref.at[part, hours_of(tm)], local_sem.at[part])
        for part in range(CHUNKS)
    ]
    own_start = pltpu.make_async_copy(start_ref, starts_ref.at[hours_of(tm)], local_sem.at[CHUNKS])
    for copy in own:
        copy.start()
    own_start.start()

    def send_cells(distance, part, index):
        return pltpu.make_async_remote_copy(
            src_ref=slab_ref.at[:, cells_of(index, part)],
            dst_ref=cells_ref.at[part, hours_of(tm)],
            send_sem=cells_send.at[part, distance],
            recv_sem=cells_recv.at[part, tm],
            device_id={"tm": index},
            device_id_type=MESH,
        )

    def take_cells(part, index):
        return pltpu.make_async_remote_copy(
            src_ref=slab_ref.at[:, cells_of(tm, part)],
            dst_ref=cells_ref.at[part, hours_of(index)],
            send_sem=cells_send.at[part, 0],
            recv_sem=cells_recv.at[part, index],
            device_id={"tm": index},
            device_id_type=MESH,
        )

    def send_start(distance, index, slot):
        return pltpu.make_async_remote_copy(
            src_ref=start_ref,
            dst_ref=starts_ref.at[hours_of(slot)],
            send_sem=starts_send.at[distance],
            recv_sem=starts_recv.at[slot],
            device_id={"tm": index},
            device_id_type=MESH,
        )

    pl.semaphore_wait(barrier, tm_count - 1 + plane - 1)

    for part in range(CHUNKS):
        for distance in order:
            send_cells(distance, part, tm_peer(distance)).start()
        if part == 0:
            for distance in order:
                send_start(distance, tm_peer(distance), tm).start()

    high_ref[...] = jnp.zeros_like(high_ref)
    low_ref[...] = jnp.zeros_like(low_ref)
    block_count = hours_all // BLOCK
    for lag, values in enumerate(toeplitz_blocks(sections_ref, block_count)):
        top = values.astype(jnp.bfloat16)
        rest = (values - top.astype(jnp.float32)).astype(jnp.bfloat16)
        for column in range(block_count - lag):
            place = (pl.ds((column + lag) * BLOCK, BLOCK), pl.ds(column * BLOCK, BLOCK))
            high_ref[place] = top
            low_ref[place] = rest

    own_start.wait()
    for distance in order:
        send_start(distance, tm_peer(distance), tm_peer(distance)).wait_recv()
    starts = starts_ref[...]

    gram_total = jnp.zeros((2 * width, 2 * width), jnp.float32)
    shares_total = jnp.zeros((hours_all, 2 * width), jnp.float32)
    half = hours_all // 2
    for part in range(CHUNKS):
        own[part].wait()
        for distance in order:
            take_cells(part, tm_peer(distance)).wait_recv()
        upper = [
            jnp.dot(ref[:half, :half], cells_ref[part, :half], preferred_element_type=jnp.float32)
            for ref in (high_ref, low_ref)
        ]
        lower = [
            jnp.dot(ref[half:], cells_ref[part], preferred_element_type=jnp.float32) for ref in (high_ref, low_ref)
        ]
        filtered = jnp.concatenate([upper[0] + upper[1], lower[0] + lower[1]], axis=0).astype(jnp.bfloat16)
        patterns = lax.dot_general(starts, filtered, (((0,), (0,)), ((), ())), preferred_element_type=jnp.float32)
        patterns_ref[:, part * chunk : (part + 1) * chunk] = patterns
        top = patterns.astype(jnp.bfloat16)
        rest = (patterns - top.astype(jnp.float32)).astype(jnp.bfloat16)
        both = jnp.concatenate([top, rest], axis=0)
        by_rows = (((1,), (1,)), ((), ()))
        gram_total = gram_total + lax.dot_general(both, both, by_rows, preferred_element_type=jnp.float32)
        shares_total = shares_total + lax.dot_general(filtered, both, by_rows, preferred_element_type=jnp.float32)

    def folded(value):
        return value + pltpu.roll(value, width, 1)

    gram_here = folded(gram_total[:width] + gram_total[width:])
    rows_each = width // tm_count
    for index in range(tm_count):
        gram_ref[index] = gram_here[index * rows_each : (index + 1) * rows_each]

    def send_gram(distance, index, slot):
        return pltpu.make_async_remote_copy(
            src_ref=gram_ref.at[index],
            dst_ref=gram_tm_ref.at[slot],
            send_sem=gram_send.at[distance],
            recv_sem=gram_recv.at[slot],
            device_id={"tm": index},
            device_id_type=MESH,
        )

    def send_shares(distance, index, slot):
        return pltpu.make_async_remote_copy(
            src_ref=shares_ref.at[index],
            dst_ref=shares_tm_ref.at[slot],
            send_sem=shares_send.at[distance],
            recv_sem=shares_recv.at[slot],
            device_id={"tm": index},
            device_id_type=MESH,
        )

    for distance in order:
        send_gram(distance, tm_peer(distance), tm).start()

    shares_here = folded(shares_total)
    left = lane_rows((hour_count // 2, 2 * width), 1) < width
    for index in range(tm_count):
        base = index * hour_count
        middle = base + hour_count // 2
        shares_ref[index] = jnp.where(left, shares_here[base:middle], shares_here[middle : base + hour_count])
    for distance in order:
        send_shares(distance, tm_peer(distance), tm).start()

    gram_tm_ref[tm] = gram_ref[tm]
    for distance in order:
        send_gram(distance, tm_peer(distance), tm_peer(distance)).wait_recv()
    gram_xy_ref[here] = jnp.sum(gram_tm_ref[...], axis=0)

    def send_far(source, slots, sends, receives, offset, slot):
        return pltpu.make_async_remote_copy(
            src_ref=source.at[here],
            dst_ref=slots.at[slot],
            send_sem=sends.at[offset],
            recv_sem=receives.at[slot],
            device_id=plane_peer(offset)[0],
            device_id_type=MESH,
        )

    far_gram = functools.partial(send_far, gram_xy_ref, gram_xy_ref, far_gram_send, far_gram_recv)
    far_shares = functools.partial(send_far, shares_xy_ref, shares_xy_ref, far_shares_send, far_shares_recv)

    def over_plane(action):
        def step(offset, carry):
            action(offset)
            return carry

        lax.fori_loop(1, plane, step, 0)

    over_plane(lambda offset: far_gram(offset, here).start())

    shares_tm_ref[tm] = shares_ref[tm]
    for distance in order:
        send_shares(distance, tm_peer(distance), tm_peer(distance)).wait_recv()
    shares_xy_ref[here] = jnp.sum(shares_tm_ref[...], axis=0)
    over_plane(lambda offset: far_shares(offset, here).start())

    over_plane(lambda offset: far_gram(offset, plane_peer(offset)[1]).wait_recv())
    gram_all_ref[tm] = jnp.sum(gram_xy_ref[...], axis=0)

    def send_all(distance, index, slot):
        return pltpu.make_async_remote_copy(
            src_ref=gram_all_ref.at[tm],
            dst_ref=gram_all_ref.at[slot],
            send_sem=all_send.at[distance],
            recv_sem=all_recv.at[slot],
            device_id={"tm": index},
            device_id_type=MESH,
        )

    for distance in order:
        send_all(distance, tm_peer(distance), tm).start()
    for distance in order:
        send_all(distance, tm_peer(distance), tm_peer(distance)).wait_recv()

    gram = gram_all_ref[...].reshape(width, 2 * width)
    shape = (width, 2 * width)
    unit = jnp.where(lane_rows(shape, 1) - width == lane_rows(shape, 0), 1.0, 0.0)
    inverse = factor_inverse(jnp.where(lane_rows(shape, 1) < width, gram, unit))[:, :width]

    scaled = inverse * math.sqrt(cells_all)
    ortho = jnp.dot(scaled, patterns_ref[...], preferred_element_type=jnp.float32, precision=FULL)
    for group in range(own_cells // LANES):
        basis_ref[group] = ortho[:, group * LANES : (group + 1) * LANES]

    over_plane(lambda offset: far_shares(offset, plane_peer(offset)[1]).wait_recv())
    packed = jnp.sum(shares_xy_ref[...], axis=0)
    shares = jnp.concatenate([packed, pltpu.roll(packed, width, 1)], axis=0)[:, :width]
    pcs_ref[...] = lax.dot_general(
        shares, inverse * math.sqrt(hours_all / cells_all), (((1,), (1,)), ((), ())),
        preferred_element_type=jnp.float32, precision=FULL,
    )

    for distance in order:
        for part in range(CHUNKS):
            send_cells(distance, part, tm_peer(distance)).wait_send()
        send_start(distance, tm_peer(distance), tm).wait_send()
        send_gram(distance, tm_peer(distance), tm).wait_send()
        send_shares(distance, tm_peer(distance), tm).wait_send()
        send_all(distance, tm_peer(distance), tm).wait_send()
    over_plane(lambda offset: far_gram(offset, here).wait_send())
    over_plane(lambda offset: far_shares(offset, here).wait_send())


def solution(mesh):
    tm_count, lat_count, lon_count = mesh.shape["tm"], mesh.shape["lat"], mesh.shape["lon"]
    plane = lat_count * lon_count

    def local(slab, start, sections):
        hour_count, cell_count = slab.shape
        width = start.shape[1]
        own_cells = cell_count // tm_count
        hours_all = hour_count * tm_count
        chunk = own_cells // CHUNKS
        rows_each = width // tm_count
        sizes = (tm_count, lat_count, lon_count, hour_count, width, own_cells)
        dma = pltpu.SemaphoreType.DMA
        f32, bf16 = jnp.float32, jnp.bfloat16
        return pl.pallas_call(
            functools.partial(kernel, sizes),
            out_shape=(
                jax.ShapeDtypeStruct((own_cells // LANES, width, LANES), f32),
                jax.ShapeDtypeStruct((hour_count, width), f32),
            ),
            in_specs=[
                pl.BlockSpec(memory_space=pl.ANY),
                pl.BlockSpec(memory_space=pl.ANY),
                pl.BlockSpec(memory_space=pltpu.SMEM),
            ],
            out_specs=(pl.BlockSpec(memory_space=pltpu.VMEM), pl.BlockSpec(memory_space=pltpu.VMEM)),
            scratch_shapes=[
                pltpu.VMEM((CHUNKS, hours_all, chunk), bf16),
                pltpu.VMEM((hours_all, width), bf16),
                pltpu.VMEM((hours_all, hours_all), bf16),
                pltpu.VMEM((hours_all, hours_all), bf16),
                pltpu.VMEM((width, own_cells), f32),
                pltpu.VMEM((tm_count, rows_each, 2 * width), f32),
                pltpu.VMEM((tm_count, rows_each, 2 * width), f32),
                pltpu.VMEM((plane, rows_each, 2 * width), f32),
                pltpu.VMEM((tm_count, rows_each, 2 * width), f32),
                pltpu.VMEM((tm_count, hour_count // 2, 2 * width), f32),
                pltpu.VMEM((tm_count, hour_count // 2, 2 * width), f32),
                pltpu.VMEM((plane, hour_count // 2, 2 * width), f32),
                dma((CHUNKS + 1,)),
                dma((CHUNKS, tm_count)), dma((CHUNKS, tm_count)),
                dma((tm_count,)), dma((tm_count,)),
                dma((tm_count,)), dma((tm_count,)),
                dma((tm_count,)), dma((tm_count,)),
                dma((plane,)), dma((plane,)),
                dma((plane,)), dma((plane,)),
                dma((tm_count,)), dma((tm_count,)),
            ],
            compiler_params=pltpu.CompilerParams(
                collective_id=0, has_side_effects=True, vmem_limit_bytes=48 * 1024 * 1024
            ),
        )(slab, start, sections)

    return jax.shard_map(
        local,
        mesh=mesh,
        in_specs=(P("tm", ("lat", "lon")), P("tm", None), P()),
        out_specs=(P(("lat", "lon", "tm"), None, None), P("tm", None)),
        check_vma=False,
    )
```

time: 379 us -> 65.7 us (0.17)
  blocking collectives: 228 us -> 0 us
  waiting for transfers between devices: 71.7 us -> 0 us
  Pallas kernels: 0 us -> 60.9 us
  between operations: 26.8 us -> 0.64 us
  matrix products: 23.6 us -> 0 us
  other arithmetic: 20 us -> 0 us
    psum x2 -> x0, blocking collectives: 203 us -> none  [the longest x1 124 us: local(): projections = lax.psum(partial_sums, ('lat', 'lon'))]
    pallas_call x0 -> x1, Pallas kernels: none -> 60.9 us  [local(): pl.pallas_call(functools.partial(kernel, sizes), out_shape=(jax.ShapeDtyp...]
    reduce_scatter x1 -> x0, waiting for transfers between devices: 41.6 us -> none  [local(): lax.psum_scatter(jnp.einsum('tk,tgc->gkc', start, block_of_rows, preferre...]
    all_gather x2 -> x0, waiting for transfers between devices: 30 us -> none  [the longest x1 29.7 us: local(): lax.all_gather(ortho.astype(jnp.bfloat16), 'tm', axis=0, tiled=True)]
    all_gather x1 -> x0, blocking collectives: 25 us -> none  [prefix(): pieces = jax.tree.map(lambda part: lax.all_gather(part, axis), value)]
    dot_general x14 -> x0, matrix products: 23.4 us -> none  [the longest x7 9.15 us: combine(): jnp.dot(subsequent[0], earlier[1], precision=TOP_PRECISION) + subsequent[1]]
    another operation x5 -> x0, other arithmetic: 12.1 us -> none  [the longest x3 6.52 us: make_orthonormal(): lower_factor = jnp.linalg.cholesky(gram_matrix)]
    unnamed x4 -> x7, local copies, waits for them, and re-layouts: 0.02 us -> 4.03 us
  transfers between devices with their start and end apart: 3 -> 0, of which waited for: 3 -> 0; matrix products, arithmetic and copies ran while one was open for 1% -> 0% of each run, Pallas kernels for 0% -> 0%
where the time goes in v1:
time: 65.7 us; the launch traced here: 65.5 us
  Pallas kernels  60.9 us (93%)
  local copies, waits for them, and re-layouts  4.03 us (6%)
    pallas_call x1, Pallas kernels, local(): pl.pallas_call(functools.partial(kernel, sizes), out_shape=(jax.ShapeDtyp...  60.9 us
    unnamed x7, local copies, waits for them, and re-layouts  4.03 us

profile of v1, /device:TPU:1, one launch (start us, length us, event | category | flops | bytes accessed | tf_op | source)
XLA Modules:
  0.0 65.5 jit_solution(11260379921410183792)
XLA Ops:
  0.6 0.8 %copy.5.sections_ref = f32[3,2]{1,0:T(4,128)S(1)} copy(f32[3,2]{0,1:T(2,128)} %param.5) | data formatting | bytes 48 | tf_op args[2]
  1.4 0.0 copy-start
  1.4 1.2 %copy-done = bf16[64,8192]{1,0:T(8,128)(2,1)S(1)} copy-done((bf16[64,8192]{1,0:T(8,128)(2,1)S(1)}, bf16[64,8192]{1,0:T(8,128)(2,1)}, u32[]{:S(2)}) %copy-start) | copy-done | bytes 1048600
  2.6 0.0 copy-start.1
  2.6 0.7 %copy-done.1 = bf16[64,64]{1,0:T(8,128)(2,1)S(1)} copy-done((bf16[64,64]{1,0:T(8,128)(2,1)S(1)}, bf16[64,64]{1,0:T(8,128)(2,1)}, u32[]{:S(2)}) %copy-start.1) | copy-done | bytes 8216
  3.3 60.9 %shard_map.50 = (f32[8,64,128]{2,1,0:T(8,128)S(1)}, f32[64,64]{1,0:T(8,128)S(1)}) custom-call(bf16[64,8192]{1,0:T(8,128)(2,1)S(1)} %copy-done, bf16[64,64]{1,0:T(8,128)(2,1)S(1)} %copy-done.1, f32[3,2]{1,0:T(4,128)S(1)} %copy.5.sections_ref), custom_call_target="tpu_custom_call" | custom-call | tf_op jit(solution)/shard_map/pallas_call | solution.py:362
  64.2 0.7 %copy.8 = f32[8,64,128]{2,1,0:T(8,128)} copy(f32[8,64,128]{2,1,0:T(8,128)S(1)} %get-tuple-element.4) | data formatting | bytes 524288
  64.9 0.6 copy.9
Async XLA Ops:
  1.4 1.2 %copy-start = (bf16[64,8192]{1,0:T(8,128)(2,1)S(1)}, bf16[64,8192]{1,0:T(8,128)(2,1)}, u32[]{:S(2)}) copy-start(bf16[64,8192]{1,0:T(8,128)(2,1)} %slab_ref.1) | copy-start | bytes 3145732
  2.6 0.7 %copy-start.1 = (bf16[64,64]{1,0:T(8,128)(2,1)S(1)}, bf16[64,64]{1,0:T(8,128)(2,1)}, u32[]{:S(2)}) copy-start(bf16[64,64]{1,0:T(8,128)(2,1)} %start_ref.1) | copy-start | bytes 24580

commit v2 on v1

v2 whole, which is shorter than its diff:
```python
import functools
import math

import jax
import jax.numpy as jnp
from jax import lax
from jax.experimental import pallas as pl
from jax.experimental.pallas import tpu as pltpu
from jax.sharding import PartitionSpec as P

LANES = 128
BLOCK = 128
CHUNKS = 4
MESH = pl.DeviceIdType.MESH
FULL = lax.Precision.HIGHEST


def lane_rows(shape, axis):
    return lax.broadcasted_iota(jnp.int32, shape, axis)


def toeplitz_blocks(sections_ref, count):
    shape = (BLOCK, BLOCK)
    offset = lane_rows(shape, 0) - lane_rows(shape, 1)
    moment = offset.astype(jnp.float32)
    totals = [jnp.zeros(shape, jnp.float32) for _ in range(count)]
    at_zero = jnp.zeros((8, LANES), jnp.float32)
    for section in range(2):
        radius = jnp.full((8, LANES), sections_ref[section, 0], jnp.float32)
        angle = jnp.full((8, LANES), sections_ref[section, 1], jnp.float32)
        amplitude = jnp.full((8, LANES), sections_ref[section, 2], jnp.float32)
        drive = amplitude * jnp.sqrt(1.0 - radius * radius)
        at_zero = at_zero + drive
        back = 1.0 / (radius * radius)
        sine, cosine = jnp.sin(angle), jnp.cos(angle)
        sine_part = drive * (1.0 - back) * cosine / sine
        cosine_part = drive * (1.0 + back)
        log_radius = jnp.log(radius)
        size = jnp.exp(moment * log_radius[:1])
        turn = moment * angle[:1]
        sine_of, cosine_of = size * jnp.sin(turn), size * jnp.cos(turn)
        for block in range(count):
            far = float(block * BLOCK)
            gain = jnp.exp(far * log_radius)
            far_sine, far_cosine = jnp.sin(far * angle), jnp.cos(far * angle)
            on_sine = gain * (sine_part * far_cosine - cosine_part * far_sine)
            on_cosine = gain * (sine_part * far_sine + cosine_part * far_cosine)
            totals[block] = totals[block] + on_sine[:1] * sine_of + on_cosine[:1] * cosine_of
    first = jnp.where(offset > 0, totals[0], jnp.where(offset == 0, at_zero[:1], 0.0))
    return [first] + totals[1:]


def factor_inverse(gram):
    width = gram.shape[0]
    count = width // 8
    rows = [gram[8 * m : 8 * m + 8] for m in range(count)]
    sub = lane_rows((8, LANES), 0)

    def spread(value, row):
        return jnp.broadcast_to(value[row : row + 1], (8, LANES))

    def step(position, rows):
        rows = list(rows)
        live = [(m < count - position).astype(jnp.float32) for m in range(count)]
        columns = [
            [jnp.broadcast_to(rows[m][:, j : j + 1], (8, LANES)) for m in range(count)] for j in range(8)
        ]
        head = rows[0]
        scale = jnp.ones((8, LANES), jnp.float32)
        scaled_rows = []
        for j in range(8):
            pivot = spread(columns[j][0], j)
            inverse_pivot = 1.0 / pivot
            scale = jnp.where(sub == j, lax.rsqrt(pivot), scale)
            columns[j][0] = jnp.where(sub > j, columns[j][0], 0.0)
            for k in range(j + 1, 8):
                weight = spread(columns[k][0], j) * inverse_pivot
                columns[k] = [ck - cj * weight for ck, cj in zip(columns[k], columns[j])]
            scaled = spread(head, j) * inverse_pivot
            scaled_rows.append(scaled)
            head = head - columns[j][0] * scaled
        out = []
        for m in range(1, count):
            taken = columns[0][m] * scaled_rows[0]
            for j in range(1, 8):
                taken = taken + columns[j][m] * scaled_rows[j]
            out.append(rows[m] - live[m] * taken)
        out.append(head * scale)
        return tuple(pltpu.roll(value, 2 * width - 8, 1) for value in out)

    rows = lax.fori_loop(0, count, step, tuple(rows))
    return jnp.concatenate(rows, axis=0)


def kernel(
    sizes,
    slab_in, start_in, sections_in,
    basis_ref, pcs_ref,
    slab_ref, start_ref, sections_ref,
    cells_ref, starts_ref, high_ref, low_ref, patterns_ref,
    gram_ref, gram_lon_ref, gram_lat_ref, gram_tm_ref, gram_all_ref,
    shares_ref, shares_tm_ref, shares_lat_ref, shares_lon_ref,
    local_sem, cells_send, cells_recv, starts_send, starts_recv,
    *stage_sems,
):
    tm_count, lat_count, lon_count, hour_count, width, own_cells = sizes
    hours_all = tm_count * hour_count
    chunk = own_cells // CHUNKS
    cells_all = own_cells * tm_count * lat_count * lon_count
    counts = {"tm": tm_count, "lat": lat_count, "lon": lon_count}
    place = {axis: lax.axis_index(axis) for axis in counts}
    tm, lat, lon = place["tm"], place["lat"], place["lon"]

    loads = [
        pltpu.make_async_copy(sections_in, sections_ref, local_sem.at[0]),
        pltpu.make_async_copy(slab_in, slab_ref, local_sem.at[1]),
        pltpu.make_async_copy(start_in, start_ref, local_sem.at[2]),
    ]
    for copy in loads:
        copy.start()

    def peer(axis, distance):
        return lax.rem(place[axis] + distance, counts[axis])

    def far_first(axis):
        count = counts[axis]
        return sorted(range(1, count), key=lambda d: -min(d, count - d))

    order = far_first("tm")
    barrier = pltpu.get_barrier_semaphore()
    for axis in ("tm", "lon", "lat"):
        for distance in far_first(axis):
            pl.semaphore_signal(barrier, inc=1, device_id={axis: peer(axis, distance)}, device_id_type=MESH)

    def hours_of(index):
        return pl.ds(pl.multiple_of(index * hour_count, hour_count), hour_count)

    def cells_of(index, part):
        return pl.ds(pl.multiple_of(index * own_cells + part * chunk, chunk), chunk)

    def send_cells(part, distance, index, slot):
        return pltpu.make_async_remote_copy(
            src_ref=slab_ref.at[:, cells_of(index, part)],
            dst_ref=cells_ref.at[part, hours_of(slot)],
            send_sem=cells_send.at[part, distance],
            recv_sem=cells_recv.at[part, slot],
            device_id={"tm": index},
            device_id_type=MESH,
        )

    def send_start(distance, index, slot):
        return pltpu.make_async_remote_copy(
            src_ref=start_ref,
            dst_ref=starts_ref.at[hours_of(slot)],
            send_sem=starts_send.at[distance],
            recv_sem=starts_recv.at[slot],
            device_id={"tm": index},
            device_id_type=MESH,
        )

    class Stage:
        def __init__(self, number, axis, source, slots):
            self.axis, self.source, self.slots = axis, source, slots
            self.sends, self.receives = stage_sems[2 * number], stage_sems[2 * number + 1]

        def copy(self, distance, slot):
            index = peer(self.axis, distance)
            return pltpu.make_async_remote_copy(
                src_ref=self.source(index),
                dst_ref=self.slots.at[slot],
                send_sem=self.sends.at[distance],
                recv_sem=self.receives.at[slot],
                device_id={self.axis: index},
                device_id_type=MESH,
            )

        def start(self):
            for distance in far_first(self.axis):
                self.copy(distance, place[self.axis]).start()

        def receive(self):
            for distance in reversed(far_first(self.axis)):
                self.copy(distance, peer(self.axis, distance)).wait_recv()

        def drain(self):
            for distance in far_first(self.axis):
                self.copy(distance, place[self.axis]).wait_send()

    gram_lon = Stage(0, "lon", lambda index: gram_ref.at[index], gram_lon_ref)
    gram_lat = Stage(1, "lat", lambda index: gram_lat_ref.at[lat], gram_lat_ref)
    gram_tm = Stage(2, "tm", lambda index: gram_tm_ref.at[tm], gram_tm_ref)
    gram_all = Stage(3, "lon", lambda index: gram_all_ref.at[lon], gram_all_ref)
    shares_tm = Stage(4, "tm", lambda index: shares_ref.at[index], shares_tm_ref)
    shares_lat = Stage(5, "lat", lambda index: shares_lat_ref.at[lat], shares_lat_ref)
    shares_lon = Stage(6, "lon", lambda index: shares_lon_ref.at[lon], shares_lon_ref)

    loads[1].wait()
    loads[2].wait()
    pl.semaphore_wait(barrier, tm_count + lat_count + lon_count - 3)

    for part in range(CHUNKS):
        for distance in order:
            send_cells(part, distance, peer("tm", distance), tm).start()
        if part == 0:
            for distance in order:
                send_start(distance, peer("tm", distance), tm).start()

    own = [
        pltpu.make_async_copy(slab_ref.at[:, cells_of(tm, part)], cells_ref.at[part, hours_of(tm)], local_sem.at[part + 3])
        for part in range(CHUNKS)
    ]
    own_start = pltpu.make_async_copy(start_ref, starts_ref.at[hours_of(tm)], local_sem.at[CHUNKS + 3])
    for copy in own:
        copy.start()
    own_start.start()
    loads[0].wait()

    high_ref[...] = jnp.zeros_like(high_ref)
    low_ref[...] = jnp.zeros_like(low_ref)
    block_count = hours_all // BLOCK
    for lag, values in enumerate(toeplitz_blocks(sections_ref, block_count)):
        top = values.astype(jnp.bfloat16)
        rest = (values - top.astype(jnp.float32)).astype(jnp.bfloat16)
        for column in range(block_count - lag):
            where = (pl.ds((column + lag) * BLOCK, BLOCK), pl.ds(column * BLOCK, BLOCK))
            high_ref[where] = top
            low_ref[where] = rest

    own_start.wait()
    for distance in order:
        send_start(distance, peer("tm", distance), peer("tm", distance)).wait_recv()
    starts = starts_ref[...]

    gram_total = jnp.zeros((2 * width, 2 * width), jnp.float32)
    shares_total = jnp.zeros((hours_all, 2 * width), jnp.float32)
    half = hours_all // 2
    for part in range(CHUNKS):
        own[part].wait()
        for distance in order:
            send_cells(part, distance, peer("tm", distance), peer("tm", distance)).wait_recv()
        upper = [
            jnp.dot(ref[:half, :half], cells_ref[part, :half], preferred_element_type=jnp.float32)
            for ref in (high_ref, low_ref)
        ]
        lower = [
            jnp.dot(ref[half:], cells_ref[part], preferred_element_type=jnp.float32) for ref in (high_ref, low_ref)
        ]
        filtered = jnp.concatenate([upper[0] + upper[1], lower[0] + lower[1]], axis=0).astype(jnp.bfloat16)
        patterns = lax.dot_general(starts, filtered, (((0,), (0,)), ((), ())), preferred_element_type=jnp.float32)
        patterns_ref[:, part * chunk : (part + 1) * chunk] = patterns
        top = patterns.astype(jnp.bfloat16)
        rest = (patterns - top.astype(jnp.float32)).astype(jnp.bfloat16)
        both = jnp.concatenate([top, rest], axis=0)
        by_rows = (((1,), (1,)), ((), ()))
        gram_total = gram_total + lax.dot_general(both, both, by_rows, preferred_element_type=jnp.float32)
        shares_total = shares_total + lax.dot_general(filtered, both, by_rows, preferred_element_type=jnp.float32)

    def folded(value):
        return value + pltpu.roll(value, width, 1)

    gram_here = folded(gram_total[:width] + gram_total[width:])
    rows_each = width // lon_count
    for index in range(lon_count):
        gram_ref[index] = gram_here[index * rows_each : (index + 1) * rows_each]
    gram_lon.start()

    shares_here = folded(shares_total)
    left = lane_rows((hour_count // 2, 2 * width), 1) < width
    for index in range(tm_count):
        base = index * hour_count
        middle = base + hour_count // 2
        shares_ref[index] = jnp.where(left, shares_here[base:middle], shares_here[middle : base + hour_count])
    shares_tm.start()
    gram_lon_ref[lon] = gram_ref[lon]
    shares_tm_ref[tm] = shares_ref[tm]

    gram_lon.receive()
    gram_lat_ref[lat] = jnp.sum(gram_lon_ref[...], axis=0)
    gram_lat.start()
    gram_lat.receive()
    gram_tm_ref[tm] = jnp.sum(gram_lat_ref[...], axis=0)
    gram_tm.start()

    shares_tm.receive()
    shares_lat_ref[lat] = jnp.sum(shares_tm_ref[...], axis=0)
    shares_lat.start()

    gram_tm.receive()
    gram_all_ref[lon] = jnp.sum(gram_tm_ref[...], axis=0)
    gram_all.start()

    shares_lat.receive()
    shares_lon_ref[lon] = jnp.sum(shares_lat_ref[...], axis=0)
    shares_lon.start()

    gram_all.receive()
    gram = gram_all_ref[...].reshape(width, 2 * width)
    shape = (width, 2 * width)
    unit = jnp.where(lane_rows(shape, 1) - width == lane_rows(shape, 0), 1.0, 0.0)
    inverse = factor_inverse(jnp.where(lane_rows(shape, 1) < width, gram, unit))[:, :width]

    scaled = inverse * math.sqrt(cells_all)
    ortho = jnp.dot(scaled, patterns_ref[...], preferred_element_type=jnp.float32, precision=FULL)
    for group in range(own_cells // LANES):
        basis_ref[group] = ortho[:, group * LANES : (group + 1) * LANES]

    shares_lon.receive()
    packed = jnp.sum(shares_lon_ref[...], axis=0)
    shares = jnp.concatenate([packed, pltpu.roll(packed, width, 1)], axis=0)[:, :width]
    pcs_ref[...] = lax.dot_general(
        shares, inverse * math.sqrt(hours_all / cells_all), (((1,), (1,)), ((), ())),
        preferred_element_type=jnp.float32, precision=FULL,
    )

    for distance in order:
        for part in range(CHUNKS):
            send_cells(part, distance, peer("tm", distance), tm).wait_send()
        send_start(distance, peer("tm", distance), tm).wait_send()
    for stage in (gram_lon, gram_lat, gram_tm, gram_all, shares_tm, shares_lat, shares_lon):
        stage.drain()


def solution(mesh):
    tm_count, lat_count, lon_count = mesh.shape["tm"], mesh.shape["lat"], mesh.shape["lon"]

    def local(slab, start, sections):
        hour_count, cell_count = slab.shape
        width = start.shape[1]
        own_cells = cell_count // tm_count
        hours_all = hour_count * tm_count
        chunk = own_cells // CHUNKS
        rows_each = width // lon_count
        sizes = (tm_count, lat_count, lon_count, hour_count, width, own_cells)
        dma = pltpu.SemaphoreType.DMA
        f32, bf16 = jnp.float32, jnp.bfloat16
        return pl.pallas_call(
            functools.partial(kernel, sizes),
            out_shape=(
                jax.ShapeDtypeStruct((own_cells // LANES, width, LANES), f32),
                jax.ShapeDtypeStruct((hour_count, width), f32),
            ),
            in_specs=[pl.BlockSpec(memory_space=pltpu.HBM)] * 3,
            out_specs=(pl.BlockSpec(memory_space=pltpu.VMEM), pl.BlockSpec(memory_space=pltpu.VMEM)),
            scratch_shapes=[
                pltpu.VMEM((hour_count, cell_count), bf16),
                pltpu.VMEM((hour_count, width), bf16),
                pltpu.SMEM(sections.shape[::-1], f32),
                pltpu.VMEM((CHUNKS, hours_all, chunk), bf16),
                pltpu.VMEM((hours_all, width), bf16),
                pltpu.VMEM((hours_all, hours_all), bf16),
                pltpu.VMEM((hours_all, hours_all), bf16),
                pltpu.VMEM((width, own_cells), f32),
                pltpu.VMEM((lon_count, rows_each, 2 * width), f32),
                pltpu.VMEM((lon_count, rows_each, 2 * width), f32),
                pltpu.VMEM((lat_count, rows_each, 2 * width), f32),
                pltpu.VMEM((tm_count, rows_each, 2 * width), f32),
                pltpu.VMEM((lon_count, rows_each, 2 * width), f32),
                pltpu.VMEM((tm_count, hour_count // 2, 2 * width), f32),
                pltpu.VMEM((tm_count, hour_count // 2, 2 * width), f32),
                pltpu.VMEM((lat_count, hour_count // 2, 2 * width), f32),
                pltpu.VMEM((lon_count, hour_count // 2, 2 * width), f32),
                dma((CHUNKS + 4,)),
                dma((CHUNKS, tm_count)), dma((CHUNKS, tm_count)),
                dma((tm_count,)), dma((tm_count,)),
            ]
            + [
                dma((count,))
                for count in (lon_count, lat_count, tm_count, lon_count, tm_count, lat_count, lon_count)
                for _ in range(2)
            ],
            compiler_params=pltpu.CompilerParams(
                collective_id=0, has_side_effects=True, vmem_limit_bytes=67043328
            ),
        )(slab, start, sections.T)

    return jax.shard_map(
        local,
        mesh=mesh,
        in_specs=(P("tm", ("lat", "lon")), P("tm", None), P()),
        out_specs=(P(("lat", "lon", "tm"), None, None), P("tm", None)),
        check_vma=False,
    )
```

time: 65.7 us -> 62.2 us (0.947)
  Pallas kernels: 60.9 us -> 59.1 us
  local copies, waits for them, and re-layouts: 4.03 us -> 2.3 us
    pallas_call x1, Pallas kernels: 60.9 us -> 59.1 us  [local(): pl.pallas_call(functools.partial(kernel, sizes), out_shape=(jax.ShapeDtyp...]
    unnamed x7 -> x4, local copies, waits for them, and re-layouts: 4.03 us -> 2.3 us
where the time goes in v2:
time: 62.2 us; the launch traced here: 62.1 us
  Pallas kernels  59.1 us (95%)
  local copies, waits for them, and re-layouts  2.3 us (4%)
  between operations  0.65 us (1%)
    pallas_call x1, Pallas kernels, local(): pl.pallas_call(functools.partial(kernel, sizes), out_shape=(jax.ShapeDtyp...  59.1 us
    unnamed x4, local copies, waits for them, and re-layouts  2.3 us

profile of v2, /device:TPU:1, one launch (start us, length us, event | category | flops | bytes accessed | tf_op | source)
XLA Modules:
  0.0 62.1 jit_solution(1823898756890364856)
XLA Ops:
  0.6 59.1 %shard_map.50 = (f32[8,64,128]{2,1,0:T(8,128)}, f32[64,64]{1,0:T(8,128)}) custom-call(bf16[64,8192]{1,0:T(8,128)(2,1)} %slab_in.1, bf16[64,64]{1,0:T(8,128)(2,1)} %start_in.1, f32[2,3]{1,0:T(2,128)} %bitcast.1), custom_call_target="tpu_custom_call" | custom-call | tf_op jit(solution)/shard_map/pallas_call | solution.py:336
  59.8 0.0 copy-start
  59.8 1.7 %copy.7 = f32[8,64,128]{2,1,0:T(8,128)} copy(f32[8,64,128]{2,1,0:T(8,128)} %get-tuple-element.4) | data formatting | bytes 524288
  61.4 0.0 copy-done
  61.4 0.6 copy.8
Async XLA Ops:
  59.8 1.7 %copy-start = (f32[64,64]{1,0:T(8,128)S(1)}, f32[64,64]{1,0:T(8,128)}, u32[]{:S(2)}) copy-start(f32[64,64]{1,0:T(8,128)} %get-tuple-element.5) | copy-start | bytes 49156
